TPU v7x, 32 devices: a whole 2x2x4 slice. The times are simulated.
32 devices in a mesh: dp: 4 (over z), expert: 8 (over y, x, core).
Axes of the slice: x: 2, y: 2, z: 4, core: 2. Of those that a mesh axis runs over, the one named last changes fastest.
Arguments:
- layer_input: bfloat16 [4096, 1024], P(('dp', 'expert')), may hold values from -6 to 6
- segment_ids: int32 [4096], P(('dp', 'expert')), may hold values from 0 to 127, never falling along the last dimension, each value on 1 to 64 neighbouring positions
- expert_routes: int32 [4096, 8], P(('dp', 'expert')), may hold values from 0 to 31, all different within a row; in each aligned block of 128 rows (0 to 127, 128 to 255, ...) at most 40 rows name the same one
- first_gain: float32 [1024], replicated, may hold values from 0.5 to 1.5
- w_query: bfloat16 [1024, 1024], P('dp'), may hold values from -0.1875 to 0.1875
- w_keyvalue: bfloat16 [1024, 1024], P('dp'), may hold values from -0.1875 to 0.1875
- w_output: bfloat16 [1024, 1024], P('dp'), may hold values from -1.5 to 1.5
- second_gain: float32 [1024], replicated, may hold values from 0.5 to 1.5
- w_router: bfloat16 [1024, 32], P('dp'), may hold values from -0.1875 to 0.1875
- w_gate_up: bfloat16 [32, 1024, 1024], P('expert', 'dp'), may hold values from -0.1875 to 0.1875
- w_down: bfloat16 [32, 512, 1024], P('expert', 'dp'), may hold values from -1 to 1
- out_cotangent: bfloat16 [4096, 1024], P(('dp', 'expert')), may hold values from -6 to 6
Outputs:
- layer_output: bfloat16 [4096, 1024], P(('dp', 'expert'))
- input_grad: bfloat16 [4096, 1024], P(('dp', 'expert'))
- first_gain_grad: float32 [1024], replicated
- query_grad: float32 [1024, 1024], P('dp')
- keyvalue_grad: float32 [1024, 1024], P('dp')
- output_grad: float32 [1024, 1024], P('dp')
- second_gain_grad: float32 [1024], replicated
- router_grad: float32 [1024, 32], P('dp')
- gate_up_grad: float32 [32, 1024, 1024], P('expert', 'dp')
- down_grad: float32 [32, 512, 1024], P('expert', 'dp')
Inputs may be any that keep to these rules, and one draw needn't show every extreme that they name: `expert_routes`: each row names 8 different experts. Among the rows of one device no expert is named by more than 40 rows, a bound that some block reaches. `segment_ids`: segment numbers never fall along the tokens; each document holds 1 to 64 tokens, and one holds exactly 64.
All inputs are finite; a program needn't handle non-finite values.
Results may differ from a plain program's by a relative error of at most 0.018.
Values may be sent and summed in bfloat16 or wider, within the bound.
No kernel may reach another device: no remote copies, remote signals or barrier semaphores. Data moves between devices by JAX's collectives and lax.ppermute only.
A program may use at most 128 MiB of HBM per device.

v0:
```python
import jax
import jax.numpy as jnp
from jax import lax
from jax.sharding import PartitionSpec as P

D = 1024
HEADS = 16
KV_HEADS = 8
HEAD_DIM = 64
F = 512
EXPERTS = 32
TOPK = 8
CAP = 40


epsilon = 1e-06
residual_scale = 0.22
score_scale = 0.015625
rope_base = 10000.0


def rope_tables(length, head_width):
    halfway = head_width // 2
    frequency = jnp.exp(
        -jnp.log(rope_base) * (2.0 * jnp.arange(halfway, dtype=jnp.float32) / head_width)
    )
    angles = jnp.arange(length, dtype=jnp.float32)[:, None] * frequency[None, :]
    cosine = jnp.concatenate([jnp.cos(angles), jnp.cos(angles)], axis=1)
    sine_table = jnp.concatenate([jnp.sin(angles), jnp.sin(angles)], axis=1)
    return (cosine, sine_table)


def rotate(values, cosine, sine_table, direction):
    halfway = values.shape[-1] // 2
    turned = jnp.concatenate([-values[..., halfway:], values[..., :halfway]], axis=-1)
    return values * cosine[:, None, :] + direction * turned * sine_table[:, None, :]


def norm_forward(inputs_f32, gain_vector):
    inverse = lax.rsqrt(jnp.mean(inputs_f32 * inputs_f32, axis=-1, keepdims=True) + epsilon)
    return (inputs_f32 * inverse * gain_vector, inverse)


def norm_backward(inputs_f32, inverse, gain_vector, upstream):
    weighted = upstream * gain_vector
    gain_part = jnp.sum(upstream * inputs_f32 * inverse, axis=0)
    through = inverse * weighted - inputs_f32 * (inverse * inverse * inverse) * jnp.mean(
        weighted * inputs_f32, axis=-1, keepdims=True
    )
    return (gain_part, through)


def activate(pre_act):
    gate_half = pre_act[..., :F]
    up_half = pre_act[..., F:]
    return gate_half * jax.nn.sigmoid(gate_half) * up_half


def activate_backward(pre_act, d_act):
    gate_half = pre_act[..., :F]
    up_half = pre_act[..., F:]
    sigmoid_gate = jax.nn.sigmoid(gate_half)
    d_gate = d_act * up_half * sigmoid_gate * (1.0 + gate_half * (1.0 - sigmoid_gate))
    d_up = d_act * gate_half * sigmoid_gate
    return jnp.concatenate([d_gate, d_up], axis=-1)


def masked_scores(query, keys, visible):
    raw_scores = (
        jnp.einsum("qkgd,pkd->kgqp", query, keys, preferred_element_type=jnp.float32) * score_scale
    )
    return jnp.where(visible[None, None], raw_scores, -1e30)


def attend_forward(normed, full_query, full_keyvalue, visible, cosine, sine_table):
    length = normed.shape[0]
    per_group = HEADS // KV_HEADS
    query_raw = jnp.dot(normed, full_query, preferred_element_type=jnp.float32).reshape(
        length, HEADS, HEAD_DIM
    )
    keyval = jnp.dot(normed, full_keyvalue, preferred_element_type=jnp.float32).reshape(
        length, 2, KV_HEADS, HEAD_DIM
    )
    query = (
        rotate(query_raw, cosine, sine_table, 1.0)
        .astype(jnp.bfloat16)
        .reshape(length, KV_HEADS, per_group, HEAD_DIM)
    )
    keys = rotate(keyval[:, 0], cosine, sine_table, 1.0).astype(jnp.bfloat16)
    values = keyval[:, 1].astype(jnp.bfloat16)
    scores = masked_scores(query, keys, visible)
    highest = jnp.max(scores, axis=-1, keepdims=True)
    log_total = highest + jnp.log(jnp.sum(jnp.exp(scores - highest), axis=-1, keepdims=True))
    probabilities = jnp.exp(scores - log_total).astype(jnp.bfloat16)
    attended = jnp.einsum(
        "kgqp,pkd->qkgd", probabilities, values, preferred_element_type=jnp.float32
    )
    attended = attended.reshape(length, HEADS * HEAD_DIM).astype(jnp.bfloat16)
    return (query, keys, values, attended, log_total)


def attend_backward(query, keys, values, attended, log_total, d_attended, visible):
    length = query.shape[0]
    per_group = HEADS // KV_HEADS
    scores = masked_scores(query, keys, visible)
    probs_f32 = jnp.exp(scores - log_total)
    probs_half = probs_f32.astype(jnp.bfloat16)
    d_att4 = d_attended.reshape(length, KV_HEADS, per_group, HEAD_DIM)
    att_four = attended.reshape(length, KV_HEADS, per_group, HEAD_DIM)
    d_values = jnp.einsum("kgqp,qkgd->pkd", probs_half, d_att4, preferred_element_type=jnp.float32)
    d_probs = jnp.einsum("qkgd,pkd->kgqp", d_att4, values, preferred_element_type=jnp.float32)
    row_delta = jnp.einsum("qkgd,qkgd->kgq", d_att4, att_four, preferred_element_type=jnp.float32)
    d_scores = (probs_f32 * (d_probs - row_delta[..., None]) * score_scale).astype(jnp.bfloat16)
    d_query = jnp.einsum(
        "kgqp,pkd->qkgd", d_scores, keys, preferred_element_type=jnp.float32
    ).reshape(length, HEADS, HEAD_DIM)
    d_keys = jnp.einsum("kgqp,qkgd->pkd", d_scores, query, preferred_element_type=jnp.float32)
    return (d_query, d_keys, d_values)


def per_device(
    layer_input,
    segment_ids,
    expert_routes,
    first_gain,
    w_query,
    w_keyvalue,
    w_output,
    second_gain,
    w_router,
    w_gate_up,
    w_down,
    out_cotangent,
):
    length = layer_input.shape[0]
    owners = lax.axis_size("expert")
    per_owner = w_gate_up.shape[0]
    full_query, full_keyvalue, full_output, full_router = (
        lax.all_gather(w_query, "dp", axis=0, tiled=True),
        lax.all_gather(w_keyvalue, "dp", axis=0, tiled=True),
        lax.all_gather(w_output, "dp", axis=0, tiled=True),
        lax.all_gather(w_router, "dp", axis=0, tiled=True),
    )
    full_gate_up, full_down = (
        lax.all_gather(w_gate_up, "dp", axis=1, tiled=True),
        lax.all_gather(w_down, "dp", axis=1, tiled=True),
    )
    cosine, sine_table = rope_tables(length, HEAD_DIM)
    places = jnp.arange(length)
    visible = (places[:, None] >= places[None, :]) & (segment_ids[:, None] == segment_ids[None, :])
    inputs_f32 = layer_input.astype(jnp.float32)
    normed, inverse = norm_forward(inputs_f32, first_gain)
    normed = normed.astype(jnp.bfloat16)
    query, keys, values, attended, log_total = attend_forward(
        normed, full_query, full_keyvalue, visible, cosine, sine_table
    )
    hidden = inputs_f32 + residual_scale * jnp.dot(
        attended, full_output, preferred_element_type=jnp.float32
    )
    normed2, inverse2 = norm_forward(hidden, second_gain)
    normed2 = normed2.astype(jnp.bfloat16)
    logits = jnp.dot(normed2, full_router, preferred_element_type=jnp.float32)
    chosen_mask = expert_routes[:, :, None] == jnp.arange(EXPERTS, dtype=jnp.int32)[None, None, :]
    chosen = jnp.sum(jnp.where(chosen_mask, logits[:, None, :], 0.0), axis=2)
    highest = jnp.max(chosen, axis=1, keepdims=True)
    exponent = jnp.exp(chosen - highest)
    gates = exponent / jnp.sum(exponent, axis=1, keepdims=True)
    onehot = chosen_mask.reshape(length * TOPK, EXPERTS).astype(jnp.int32)
    ranking = jnp.sum((jnp.cumsum(onehot, axis=0) - 1) * onehot, axis=1)
    target = expert_routes.reshape(length * TOPK) * CAP + ranking
    pair_slot = (
        jnp.full((EXPERTS * CAP,), length * TOPK, jnp.int32)
        .at[target]
        .set(jnp.arange(length * TOPK, dtype=jnp.int32))
    )
    token_slot = pair_slot // TOPK
    padded_normed = jnp.concatenate([normed2, jnp.zeros((1, D), jnp.bfloat16)], axis=0)
    outgoing = padded_normed[token_slot].reshape(EXPERTS, CAP, D)
    piece = lax.all_to_all(outgoing, "expert", split_axis=0, concat_axis=0, tiled=True)
    slots = piece.shape[1]
    grouped = piece.reshape(owners, per_owner, slots, D)
    pre_act = jnp.einsum(
        "sjnd,jdf->sjnf", grouped, full_gate_up, preferred_element_type=jnp.float32
    )
    activated = activate(pre_act).astype(jnp.bfloat16)
    result = jnp.einsum(
        "sjnf,jfd->sjnd", activated, full_down, preferred_element_type=jnp.float32
    ).astype(jnp.bfloat16)
    expert_out = result.reshape(owners * per_owner, slots, D)
    kept_pre = pre_act.reshape(owners * per_owner, slots, 2 * F)
    kept_act = activated.reshape(owners * per_owner, slots, F)
    returned = lax.all_to_all(expert_out, "expert", split_axis=0, concat_axis=0, tiled=True)
    picked = returned.reshape(EXPERTS * CAP, D)[target].reshape(length, TOPK, D).astype(jnp.float32)
    combined = jnp.sum(gates[:, :, None] * picked, axis=1)
    layer_output = (hidden + residual_scale * combined).astype(jnp.bfloat16)
    d_out = out_cotangent.astype(jnp.float32)
    d_gates = residual_scale * jnp.sum(picked * d_out[:, None, :], axis=2)
    d_chosen = gates * (d_gates - jnp.sum(gates * d_gates, axis=1, keepdims=True))
    d_logits = jnp.sum(jnp.where(chosen_mask, d_chosen[:, :, None], 0.0), axis=1).astype(
        jnp.bfloat16
    )
    d_router = jnp.dot(normed2.T, d_logits, preferred_element_type=jnp.float32)
    d_pairs = (
        (residual_scale * gates[:, :, None] * d_out[:, None, :])
        .astype(jnp.bfloat16)
        .reshape(length * TOPK, D)
    )
    padded_pairs = jnp.concatenate([d_pairs, jnp.zeros((1, D), jnp.bfloat16)], axis=0)
    outgoing_grad = padded_pairs[pair_slot].reshape(EXPERTS, CAP, D)
    arrived_grad = lax.all_to_all(outgoing_grad, "expert", split_axis=0, concat_axis=0, tiled=True)
    grouped_grad = arrived_grad.reshape(owners, per_owner, CAP, D)
    grouped_rows = piece.reshape(owners, per_owner, CAP, D)
    pre_act = kept_pre.reshape(owners, per_owner, CAP, 2 * F)
    activated = kept_act.reshape(owners, per_owner, CAP, F)
    d_act = jnp.einsum(
        "sjnd,jfd->sjnf", grouped_grad, full_down, preferred_element_type=jnp.float32
    )
    d_down = jnp.einsum(
        "sjnf,sjnd->jfd", activated, grouped_grad, preferred_element_type=jnp.float32
    )
    d_pre = activate_backward(pre_act, d_act).astype(jnp.bfloat16)
    d_gate_up = jnp.einsum(
        "sjnd,sjnf->jdf", grouped_rows, d_pre, preferred_element_type=jnp.float32
    )
    d_rows = jnp.einsum(
        "sjnf,jdf->sjnd", d_pre, full_gate_up, preferred_element_type=jnp.float32
    ).astype(jnp.bfloat16)
    back_rows = lax.all_to_all(
        d_rows.reshape(owners * per_owner, CAP, D),
        "expert",
        split_axis=0,
        concat_axis=0,
        tiled=True,
    )
    gate_up_grad, down_grad = (
        lax.psum_scatter(
            d_gate_up.astype(jnp.bfloat16), "dp", scatter_dimension=1, tiled=True
        ).astype(jnp.float32),
        lax.psum_scatter(d_down.astype(jnp.bfloat16), "dp", scatter_dimension=1, tiled=True).astype(
            jnp.float32
        ),
    )
    gathered_back = (
        back_rows.reshape(EXPERTS * CAP, D)[target].reshape(length, TOPK, D).astype(jnp.float32)
    )
    d_normed2 = jnp.sum(gathered_back, axis=1) + jnp.dot(
        d_logits, full_router.T, preferred_element_type=jnp.float32
    )
    d_second_gain, d_through = norm_backward(hidden, inverse2, second_gain, d_normed2)
    d_hidden = d_out + d_through
    d_branch = (residual_scale * d_hidden).astype(jnp.bfloat16)
    d_wout = jnp.dot(attended.T, d_branch, preferred_element_type=jnp.float32)
    d_attended = jnp.dot(d_branch, full_output.T, preferred_element_type=jnp.float32).astype(
        jnp.bfloat16
    )
    d_query, d_keys, d_values = attend_backward(
        query, keys, values, attended, log_total, d_attended, visible
    )
    d_query = (
        rotate(d_query, cosine, sine_table, -1.0)
        .reshape(length, HEADS * HEAD_DIM)
        .astype(jnp.bfloat16)
    )
    d_keys = rotate(d_keys, cosine, sine_table, -1.0)
    d_keyvalue = (
        jnp.stack([d_keys, d_values], axis=1)
        .reshape(length, 2 * KV_HEADS * HEAD_DIM)
        .astype(jnp.bfloat16)
    )
    d_wquery = jnp.dot(normed.T, d_query, preferred_element_type=jnp.float32)
    d_wkeyvalue = jnp.dot(normed.T, d_keyvalue, preferred_element_type=jnp.float32)
    d_normed = jnp.dot(d_query, full_query.T, preferred_element_type=jnp.float32) + jnp.dot(
        d_keyvalue, full_keyvalue.T, preferred_element_type=jnp.float32
    )
    d_first_gain, d_inputs = norm_backward(inputs_f32, inverse, first_gain, d_normed)
    input_grad = (d_hidden + d_inputs).astype(jnp.bfloat16)
    share_query, share_keyvalue, share_output, share_router = (
        lax.psum_scatter(
            d_wquery.astype(jnp.bfloat16), "dp", scatter_dimension=0, tiled=True
        ).astype(jnp.float32),
        lax.psum_scatter(
            d_wkeyvalue.astype(jnp.bfloat16), "dp", scatter_dimension=0, tiled=True
        ).astype(jnp.float32),
        lax.psum_scatter(d_wout.astype(jnp.bfloat16), "dp", scatter_dimension=0, tiled=True).astype(
            jnp.float32
        ),
        lax.psum_scatter(
            d_router.astype(jnp.bfloat16), "dp", scatter_dimension=0, tiled=True
        ).astype(jnp.float32),
    )
    query_grad, keyvalue_grad, output_grad, router_grad = (
        lax.psum(share_query.astype(jnp.bfloat16), "expert").astype(jnp.float32),
        lax.psum(share_keyvalue.astype(jnp.bfloat16), "expert").astype(jnp.float32),
        lax.psum(share_output.astype(jnp.bfloat16), "expert").astype(jnp.float32),
        lax.psum(share_router.astype(jnp.bfloat16), "expert").astype(jnp.float32),
    )
    first_gain_grad, second_gain_grad = lax.psum((d_first_gain, d_second_gain), ("dp", "expert"))
    return (
        layer_output,
        input_grad,
        first_gain_grad,
        query_grad,
        keyvalue_grad,
        output_grad,
        second_gain_grad,
        router_grad,
        gate_up_grad,
        down_grad,
    )


def solution(mesh):
    return jax.shard_map(
        per_device,
        mesh=mesh,
        in_specs=(
            P(("dp", "expert"), None),
            P(("dp", "expert")),
            P(("dp", "expert"), None),
            P(),
            P("dp", None),
            P("dp", None),
            P("dp", None),
            P(),
            P("dp", None),
            P("expert", "dp", None),
            P("expert", "dp", None),
            P(("dp", "expert"), None),
        ),
        out_specs=(
            P(("dp", "expert"), None),
            P(("dp", "expert"), None),
            P(),
            P("dp", None),
            P("dp", None),
            P("dp", None),
            P(),
            P("dp", None),
            P("expert", "dp", None),
            P("expert", "dp", None),
        ),
        check_vma=False,
    )
```

profile of v0, /device:TPU:0, one launch (start us, length us, event | category | flops | bytes accessed | tf_op | source)
XLA Modules:
  0.0 949.3 jit_solution(3258476665702379429)
XLA Ops:
  12.7 9.0 reduce-window.6
  22.8 4.3 scatter_custom_fusion
  27.2 30.9 %all-gather.6.cloned.1.call-done = bf16[1024,1024]{1,0:T(8,128)(2,1)} async-done(((bf16[256,1024]{1,0:T(8,128)(2,1)}), bf16[1024,1024]{1,0:T(8,128)(2,1)}) %all-gather.6.cloned.1.call-update) | async-done | bytes 2097168 | tf_op jit(solution)/shard_map/all_gather | solution.py:140
  58.1 2.6 fusion.85
  60.7 43.4 %all-gather.8.cloned.1.call-done = bf16[1024,1024]{1,0:T(8,128)(2,1)} async-done(((bf16[256,1024]{1,0:T(8,128)(2,1)}), bf16[1024,1024]{1,0:T(8,128)(2,1)}) %all-gather.8.cloned.1.call-update) | async-done | bytes 2097168 | tf_op jit(solution)/shard_map/all_gather | solution.py:139
  104.1 2.6 fusion.83
  108.6 41.6 %all-gather.10.cloned.1.call-done = bf16[1024,1024]{1,0:T(8,128)(2,1)} async-done(((bf16[256,1024]{1,0:T(8,128)(2,1)}), bf16[1024,1024]{1,0:T(8,128)(2,1)}) %all-gather.10.cloned.1.call-update) | async-done | bytes 2097168 | tf_op jit(solution)/shard_map/all_gather | solution.py:141
  150.2 2.2 multiply_reduce_fusion.2
  153.3 5.1 gather_fusion
  158.4 4.6 all-to-all-start
  163.0 15.7 %all_gather.21 = bf16[1024,32]{0,1:T(8,128)(2,1)S(1)} all-gather(bf16[256,32]{0,1:T(8,128)(2,1)S(1)} %copy-done.34), channel_id=1, replica_groups=mesh['dp'=4,'expert'=8] {'dp'}, dimensions={0}, use_global_device_ids=true | all-gather | bytes 81920 | tf_op jit(solution)/shard_map/all_gather | solution.py:142
  179.8 5.1 gather_fusion.2
  184.9 10.3 %all-to-all-done = bf16[32,40,1024]{2,1,0:T(8,128)(2,1)} async-done(((bf16[32,40,1024]{2,1,0:T(8,128)(2,1)}), bf16[32,40,1024]{2,1,0:T(8,128)(2,1)}, u32[]{:S(2)}, u32[]{:S(2)}) %all-to-all-start) | async-done | bytes 2621472 | tf_op jit(solution)/shard_map/all_to_all | solution.py:179
  195.2 3.8 all-to-all-start.2
  199.0 102.1 %all-gather.12.cloned.1.call-done = bf16[4,1024,1024]{2,1,0:T(8,128)(2,1)} async-done(((bf16[4,256,1024]{2,1,0:T(8,128)(2,1)}), bf16[4,1024,1024]{2,1,0:T(8,128)(2,1)}) %all-gather.12.cloned.1.call-update) | async-done | bytes 8388624 | tf_op jit(solution)/shard_map/all_gather | solution.py:145
  301.1 9.5 fusion.18
  310.6 70.9 %all-gather.14.cloned.1.call-done = bf16[4,512,1024]{2,1,0:T(8,128)(2,1)} async-done(((bf16[4,128,1024]{2,1,0:T(8,128)(2,1)}), bf16[4,512,1024]{2,1,0:T(8,128)(2,1)}) %all-gather.14.cloned.1.call-update) | async-done | bytes 4194320 | tf_op jit(solution)/shard_map/all_gather | solution.py:146
  381.4 7.6 fusion.13
  389.0 10.1 %convert_bitcast_fusion = bf16[8,4,40,1024]{3,2,0,1:T(8,128)(2,1)S(1)} fusion(bf16[4,1024,1024]{2,1,0:T(8,128)(2,1)} %all-gather.12.cloned.1.call-done, bf16[8,4,40,512]{3,2,0,1:T(8,128)(2,1)S(1)} %get-tuple-element.24, bf16[8,4,40,512]{3,2,0,1:T(8,128)(2,1)S(1)} %get-tuple-element.23), kind=kOutput, calls=%fused_computation.32 | convolution fusion | flops 2690908160 | bytes 13631488 | tf_op jit(solution)/shard_map/sjnf,jdf->sjnd/dot_general | solution.py:225
  399.2 1.8 copy.91
  401.0 3.7 all-to-all-start.3
  404.7 4.1 convert_bitcast_fusion.1
  408.8 1.9 copy.88
  410.7 26.2 %all-to-all-done.3 = bf16[32,40,1024]{2,1,0:T(8,128)(2,1)S(1)} async-done(((bf16[32,40,1024]{2,1,0:T(8,128)(2,1)}), bf16[32,40,1024]{2,1,0:T(8,128)(2,1)S(1)}, u32[]{:S(2)}, u32[]{:S(2)}) %all-to-all-start.3) | async-done | bytes 2621472 | tf_op jit(solution)/shard_map/all_to_all | solution.py:228
  436.9 4.4 all-to-all-start.1
  441.6 1.3 broadcast_clamp_fusion
  442.9 0.7 copy.81
  443.6 5.6 gather_fusion.3
  449.2 3.8 convert_reduce_fusion
  453.0 20.6 %all-to-all-done.1 = bf16[32,40,1024]{2,1,0:T(8,128)(2,1)} async-done(((bf16[32,40,1024]{2,1,0:T(8,128)(2,1)}), bf16[32,40,1024]{2,1,0:T(8,128)(2,1)}, u32[]{:S(2)}, u32[]{:S(2)}) %all-to-all-start.1) | async-done | bytes 2621472 | tf_op jit(solution)/shard_map/all_to_all | solution.py:192
  473.6 7.1 gather_fusion.1
  480.7 2.4 fusion.5
  483.1 1.0 copy.92
  484.9 2.2 multiply_reduce_fusion
  487.2 2.2 subtract_add_fusion
  489.4 0.8 copy-done.6
  490.2 1.5 convolution_convert_fusion.3
  491.7 1.1 copy.93
  492.8 1.0 fusion.53
  493.9 1.4 fusion.34
  495.9 2.1 convolution_convert_fusion.2
  498.9 2.1 convolution_convert_fusion.1
  501.1 2.0 convolution_convert_fusion
  503.2 0.8 convolution_convert_fusion.5
  504.1 34.5 %reduce-scatter.7.cloned.1.call-done = bf16[256,1024]{1,0:T(8,128)(2,1)} async-done(((bf16[1024,1024]{1,0:T(8,128)(2,1)}), bf16[256,1024]{1,0:T(8,128)(2,1)}) %reduce-scatter.7.cloned.1.call-update) | async-done | bytes 524304 | tf_op jit(solution)/shard_map/reduce_scatter | solution.py:278
  538.6 45.7 %reduce-scatter.9.cloned.1.call-done = bf16[256,1024]{1,0:T(8,128)(2,1)} async-done(((bf16[1024,1024]{1,0:T(8,128)(2,1)}), bf16[256,1024]{1,0:T(8,128)(2,1)}) %reduce-scatter.9.cloned.1.call-update) | async-done | bytes 524304 | tf_op jit(solution)/shard_map/reduce_scatter | solution.py:281
  584.3 45.1 %reduce-scatter.11.cloned.1.call-done = bf16[256,1024]{1,0:T(8,128)(2,1)} async-done(((bf16[1024,1024]{1,0:T(8,128)(2,1)}), bf16[256,1024]{1,0:T(8,128)(2,1)}) %reduce-scatter.11.cloned.1.call-update) | async-done | bytes 524304 | tf_op jit(solution)/shard_map/reduce_scatter | solution.py:284
  629.5 6.1 bitcast_convert_fusion.1
  636.0 1.0 copy-done.40
  636.9 9.9 %bitcast_convert_fusion = bf16[4,1024,1024]{2,1,0:T(8,128)(2,1)} fusion(bf16[8,4,40,1024]{3,2,1,0:T(8,128)(2,1)} %bitcast.21, bf16[8,4,40,512]{3,2,0,1:T(8,128)(2,1)} %copy-done.41, bf16[8,4,40,512]{3,2,0,1:T(8,128)(2,1)S(1)} %copy-done.40), kind=kOutput, calls=%fused_computation.5 | convolution fusion | flops 2693791744 | bytes 13631488 | tf_op jit(solution)/shard_map/sjnd,sjnf->jdf/dot_general | solution.py:222
  646.9 1.6 copy-done.4
  648.5 0.8 fusion.91
  649.3 0.8 copy-done.3
  650.0 1.0 fusion.48
  651.0 39.6 %all-reduce.2 = (f32[1024]{0:T(1024)}, f32[1024]{0:T(1024)}) all-reduce(f32[1024]{0:T(1024)S(1)} %get-tuple-element.14, f32[1024]{0:T(1024)S(1)} %copy-done.33), channel_id=1, replica_groups=mesh['dp'=4,'expert'=8] {'dp','expert'}, use_global_device_ids=true, to_apply=%region_19.20 | all-reduce | flops 2048 | bytes 16384 | tf_op jit(solution)/shard_map/psum | solution.py:297
  690.7 0.9 fusion.45
  691.6 23.8 %psum.47 = bf16[256,32]{0,1:T(8,128)(2,1)S(1)} all-reduce(bf16[256,32]{0,1:T(8,128)(2,1)} %reduce-scatter.13.cloned.1.call-done), channel_id=1, replica_groups=mesh['dp'=4,'expert'=8] {'expert'}, use_global_device_ids=true, to_apply=%region_29.30 | all-reduce | flops 8192 | bytes 32768 | tf_op jit(solution)/shard_map/psum | solution.py:295
  716.0 2.2 convert_element_type.179
  718.2 2.1 convert_element_type.181
  720.3 1.1 convert_element_type.183
  721.4 69.1 %reduce-scatter.17.cloned.1.call-done = bf16[4,128,1024]{2,1,0:T(8,128)(2,1)} async-done(((bf16[4,512,1024]{2,1,0:T(8,128)(2,1)}), bf16[4,128,1024]{2,1,0:T(8,128)(2,1)}) %reduce-scatter.17.cloned.1.call-update) | async-done | bytes 1048592 | tf_op jit(solution)/shard_map/reduce_scatter | solution.py:239
  790.5 2.8 convert_element_type.189
  793.3 144.6 %reduce-scatter.15.cloned.1.call-done = bf16[4,256,1024]{2,1,0:T(8,128)(2,1)} async-done(((bf16[4,1024,1024]{2,1,0:T(8,128)(2,1)}), bf16[4,256,1024]{2,1,0:T(8,128)(2,1)}) %reduce-scatter.15.cloned.1.call-update) | async-done | bytes 2097168 | tf_op jit(solution)/shard_map/reduce_scatter | solution.py:236
  937.9 4.1 convert_element_type.187
  (169 shorter events, 14.0 us)
Async XLA Ops:
  7.2 3.4 copy-start.28
  7.2 3.7 copy-start.2
  7.2 5.2 copy-start.37
  7.2 50.9 %all-gather.6.cloned.1.call-start = ((), (), s32[]{:S(2)}) async-start(), calls=%async_computation.10 | async-start | bytes 2621440 | tf_op jit(solution)/shard_map/all_gather | solution.py:140
  7.9 96.2 %all-gather.8.cloned.1.call-start = ((), (), s32[]{:S(2)}) async-start(), calls=%async_computation.11 | async-start | bytes 2621440 | tf_op jit(solution)/shard_map/all_gather | solution.py:139
  8.7 141.5 %all-gather.10.cloned.1.call-start = ((), (), s32[]{:S(2)}) async-start(), calls=%async_computation.12 | async-start | bytes 2621440 | tf_op jit(solution)/shard_map/all_gather | solution.py:141
  9.4 48.7 %copy-start.25 = (f32[1024]{0:T(1024)S(1)}, f32[1024]{0:T(1024)}, u32[]{:S(2)}) copy-start(f32[1024]{0:T(1024)} %param.15) | copy-start | bytes 12292
  9.4 291.6 %all-gather.12.cloned.1.call-start = ((), (), s32[]{:S(2)}) async-start(), calls=%async_computation.13 | async-start | bytes 10485760 | tf_op jit(solution)/shard_map/all_gather | solution.py:145
  10.0 371.4 %all-gather.14.cloned.1.call-start = ((), (), s32[]{:S(2)}) async-start(), calls=%async_computation.14 | async-start | bytes 5242880 | tf_op jit(solution)/shard_map/all_gather | solution.py:146
  11.6 92.5 %copy-start.31 = (f32[128]{0:T(128)}, f32[128]{0:T(128)S(1)}, u32[]{:S(2)}) copy-start(f32[128]{0:T(128)S(1)} %get-tuple-element.41) | copy-start | bytes 1540
  12.4 94.4 %copy-start.19 = (f32[128,64]{0,1:T(8,128)}, f32[128,64]{0,1:T(8,128)S(1)}, u32[]{:S(2)}) copy-start(f32[128,64]{0,1:T(8,128)S(1)} %pad_maximum_fusion.2) | copy-start | bytes 98308
  22.2 0.6 copy-start.35
  60.7 46.9 %copy-start.9 = (f32[128,1024]{0,1:T(8,128)}, f32[128,1024]{0,1:T(8,128)S(1)}, u32[]{:S(2)}) copy-start(f32[128,1024]{0,1:T(8,128)S(1)} %fusion.85) | copy-start | bytes 1572868
  106.8 0.7 copy-start.15
  107.3 1.0 copy-start
  107.4 45.7 %copy-start.29 = (f32[1024]{0:T(1024)S(1)}, f32[1024]{0:T(1024)}, u32[]{:S(2)}) copy-start(f32[1024]{0:T(1024)} %param.19) | copy-start | bytes 12292
  108.6 44.3 %copy-start.12 = (bf16[8,64,2,128]{3,1,2,0:T(8,128)(2,1)}, bf16[8,64,2,128]{3,1,2,0:T(8,128)(2,1)S(1)}, u32[]{:S(2)}) copy-start(bf16[8,64,2,128]{3,1,2,0:T(8,128)(2,1)S(1)} %convolution_convert_fusion.4) | copy-start | bytes 786436
  152.3 0.8 copy-start.8
  152.9 5.5 copy-start.36
  153.3 25.5 %copy-start.10 = (bf16[128,1024]{1,0:T(8,128)(2,1)}, bf16[128,1024]{1,0:T(8,128)(2,1)S(1)}, u32[]{:S(2)}) copy-start(bf16[128,1024]{1,0:T(8,128)(2,1)S(1)} %multiply_convert_fusion.2) | copy-start | bytes 786436
  158.4 4.6 copy-start.18
  158.4 4.7 copy-start.34
  158.4 36.8 %all-to-all-start = ((bf16[32,40,1024]{2,1,0:T(8,128)(2,1)}), bf16[32,40,1024]{2,1,0:T(8,128)(2,1)}, u32[]{:S(2)}, u32[]{:S(2)}) async-start(bf16[32,40,1024]{2,1,0:T(8,128)(2,1)} %bitcast.20), calls=%async_computation | async-start | bytes 5242880 | tf_op jit(solution)/shard_map/all_to_all | solution.py:179
  178.7 0.6 copy-start.21
  195.2 115.4 %all-to-all-start.2 = ((bf16[32,40,1024]{2,1,0:T(8,128)(2,1)}), bf16[32,40,1024]{2,1,0:T(8,128)(2,1)S(1)}, u32[]{:S(2)}, u32[]{:S(2)}) async-start(bf16[32,40,1024]{2,1,0:T(8,128)(2,1)} %bitcast.195), calls=%async_computation.2 | async-start | bytes 5242880 | tf_op jit(solution)/shard_map/all_to_all | solution.py:210
  310.6 78.5 %copy-start.14 = (bf16[32,40,1024]{2,1,0:T(8,128)(2,1)}, bf16[32,40,1024]{2,1,0:T(8,128)(2,1)S(1)}, u32[]{:S(2)}) copy-start(bf16[32,40,1024]{2,1,0:T(8,128)(2,1)S(1)} %all-to-all-done.2) | copy-start | bytes 7864324
  389.0 10.1 %copy-start.39 = (bf16[8,4,40,512]{3,2,0,1:T(8,128)(2,1)}, bf16[8,4,40,512]{3,2,0,1:T(8,128)(2,1)S(1)}, u32[]{:S(2)}) copy-start(bf16[8,4,40,512]{3,2,0,1:T(8,128)(2,1)S(1)} %get-tuple-element.23) | copy-start | bytes 3932164
  389.0 10.2 %copy-start.41 = (bf16[8,4,40,512]{3,2,0,1:T(8,128)(2,1)}, bf16[8,4,40,512]{3,2,0,1:T(8,128)(2,1)S(1)}, u32[]{:S(2)}) copy-start(bf16[8,4,40,512]{3,2,0,1:T(8,128)(2,1)S(1)} %get-tuple-element.24) | copy-start | bytes 3932164
  401.0 35.9 %all-to-all-start.3 = ((bf16[32,40,1024]{2,1,0:T(8,128)(2,1)}), bf16[32,40,1024]{2,1,0:T(8,128)(2,1)S(1)}, u32[]{:S(2)}, u32[]{:S(2)}) async-start(bf16[32,40,1024]{2,1,0:T(8,128)(2,1)} %bitcast.194), calls=%async_computation.3 | async-start | bytes 5242880 | tf_op jit(solution)/shard_map/all_to_all | solution.py:228
  436.9 36.6 %all-to-all-start.1 = ((bf16[32,40,1024]{2,1,0:T(8,128)(2,1)}), bf16[32,40,1024]{2,1,0:T(8,128)(2,1)}, u32[]{:S(2)}, u32[]{:S(2)}) async-start(bf16[32,40,1024]{2,1,0:T(8,128)(2,1)} %bitcast.193), calls=%async_computation.1 | async-start | bytes 5242880 | tf_op jit(solution)/shard_map/all_to_all | solution.py:192
  441.3 97.2 %reduce-scatter.7.cloned.1.call-start = ((), (), s32[]{:S(2)}) async-start(), calls=%async_computation.15 | async-start | bytes 2621440 | tf_op jit(solution)/shard_map/reduce_scatter | solution.py:278
  449.2 24.4 %copy-start.30 = (s32[1024]{0:T(1024)S(1)}, s32[1024]{0:T(1024)}, u32[]{:S(2)}) copy-start(s32[1024]{0:T(1024)} %broadcast_clamp_fusion) | copy-start | bytes 12292
  473.6 7.1 copy-start.24
  483.1 7.1 copy-start.5
  484.9 2.2 copy-start.26
  489.4 0.8 copy-start.6
  489.4 4.5 copy-start.1
  491.7 3.9 copy-start.23
  493.9 1.7 copy-start.20
  495.3 0.6 copy-start.32
  495.9 2.2 copy-start.16
  498.0 86.2 %reduce-scatter.9.cloned.1.call-start = ((), (), s32[]{:S(2)}) async-start(), calls=%async_computation.16 | async-start | bytes 2621440 | tf_op jit(solution)/shard_map/reduce_scatter | solution.py:281
  498.8 2.3 copy-start.7
  498.8 2.3 copy-start.13
  501.0 2.2 copy-start.11
  501.0 2.2 copy-start.27
  501.0 128.4 %reduce-scatter.11.cloned.1.call-start = ((), (), s32[]{:S(2)}) async-start(), calls=%async_computation.17 | async-start | bytes 2621440 | tf_op jit(solution)/shard_map/reduce_scatter | solution.py:284
  503.1 126.4 %copy-start.17 = (bf16[8,4,40,512]{3,2,0,1:T(8,128)(2,1)S(1)}, bf16[8,4,40,512]{3,2,0,1:T(8,128)(2,1)}, u32[]{:S(2)}) copy-start(bf16[8,4,40,512]{3,2,0,1:T(8,128)(2,1)} %get-tuple-element.25) | copy-start | bytes 3932164
  503.2 188.4 %reduce-scatter.13.cloned.1.call-start = ((), (), s32[]{:S(2)}) async-start(), calls=%async_computation.18 | async-start | bytes 81920 | tf_op jit(solution)/shard_map/reduce_scatter | solution.py:287
  504.1 212.0 %all-reduce.6.cloned.1.call-start = ((), (), s32[]{:S(2)}) async-start(), calls=%async_computation.21 | async-start | bytes 3145728 | tf_op jit(solution)/shard_map/psum | solution.py:292
  629.5 161.1 %reduce-scatter.17.cloned.1.call-start = ((), (), s32[]{:S(2)}) async-start(), calls=%async_computation.20 | async-start | bytes 5242880 | tf_op jit(solution)/shard_map/reduce_scatter | solution.py:239
  635.6 1.3 copy-start.40
  635.7 302.3 %reduce-scatter.15.cloned.1.call-start = ((), (), s32[]{:S(2)}) async-start(), calls=%async_computation.19 | async-start | bytes 10485760 | tf_op jit(solution)/shard_map/reduce_scatter | solution.py:236
  646.9 1.6 copy-start.4
  648.4 1.6 copy-start.3
  648.4 2.6 copy-start.33
  648.4 42.2 %copy-start.38 = (f32[128]{0:T(128)S(1)}, f32[128]{0:T(128)}, u32[]{:S(2)}) copy-start(f32[128]{0:T(128)} %get-tuple-element.40) | copy-start | bytes 1540
  716.0 4.3 copy-start.22
Sparse Core Ops, SparseCore 0:
  9.6 48.4 all-gather.5
  59.7 44.4 all-gather.7
  105.7 44.4 all-gather.9
  151.6 149.4 all-gather.11
  302.5 78.9 all-gather.13
  498.2 40.3 reduce-scatter.6
  541.4 42.8 reduce-scatter.8
  586.6 42.8 reduce-scatter.10
  632.2 18.4 reduce-scatter.12
  654.1 57.3 all-reduce.5
  714.4 76.0 reduce-scatter.16
  792.8 145.1 reduce-scatter.14
where the time goes:
time: 957 us; the launch traced here: 949 us
  waiting for transfers between devices  688 us (72%)
  blocking collectives  79.1 us (8%)
  matrix products  70.4 us (7%)
  local copies, waits for them, and re-layouts  41 us (4%)
  other arithmetic  37.8 us (4%)
  starting transfers between devices  17.4 us (2%)
  between operations  15.4 us (2%)
    reduce_scatter x1, waiting for transfers between devices, per_device(): lax.psum_scatter(d_gate_up.astype(jnp.bfloat16), 'dp', scatter_dimension=...  145 us
    all_gather x1, waiting for transfers between devices, per_device(): lax.all_gather(w_gate_up, 'dp', axis=1, tiled=True)  102 us
    all_gather x1, waiting for transfers between devices, per_device(): lax.all_gather(w_down, 'dp', axis=1, tiled=True)  70.9 us
    reduce_scatter x1, waiting for transfers between devices, per_device(): lax.psum_scatter(d_down.astype(jnp.bfloat16), 'dp', scatter_dimension=1,...  69.1 us
    reduce_scatter x1, waiting for transfers between devices, per_device(): lax.psum_scatter(d_wkeyvalue.astype(jnp.bfloat16), 'dp', scatter_dimensio...  45.7 us
    reduce_scatter x1, waiting for transfers between devices, per_device(): lax.psum_scatter(d_wout.astype(jnp.bfloat16), 'dp', scatter_dimension=0,...  45.1 us
    all_gather x1, waiting for transfers between devices, per_device(): lax.all_gather(w_query, 'dp', axis=0, tiled=True)  43.4 us
    all_gather x1, waiting for transfers between devices, per_device(): lax.all_gather(w_output, 'dp', axis=0, tiled=True)  41.6 us
  transfers between devices with their start and end apart: 16, of which 13 were waited for; matrix products, arithmetic and copies ran while one was open for 10% of the time, Pallas kernels for 0%

commit v1 on v0

--- a/solution.py
+++ b/solution.py
@@ -118,6 +118,72 @@
     return (d_query, d_keys, d_values)
 
 
+def butterfly_sum(value, axes):
+    for axis in axes:
+        size = lax.axis_size(axis)
+        step = 1
+        while step < size:
+            value = value + lax.ppermute(value, axis, [(i, i ^ step) for i in range(size)])
+            step *= 2
+    return value
+
+
+def spread_over(axes, array):
+    for axis in reversed(axes):
+        array = lax.all_gather(array, axis, axis=0, tiled=True)
+    return array
+
+
+def sum_to_owner(axes, array):
+    for axis in axes:
+        array = lax.psum_scatter(array, axis, scatter_dimension=0, tiled=True)
+    return array
+
+
+def expert_pass(tokens, cotangents, gate, hit, w_up, w_dn):
+    blocks = tokens.shape[0] // 128
+    ranking = jnp.cumsum(hit.reshape(blocks, 128).astype(jnp.int32), axis=1) - 1
+    slot = jnp.where(hit.reshape(blocks, 128), ranking, -1)
+    select = slot[:, None, :] == jnp.arange(CAP, dtype=jnp.int32)[None, :, None]
+    onehot = select.astype(jnp.bfloat16)
+    rows = blocks * CAP
+    picked = jnp.einsum(
+        "bst,btd->bsd", onehot, tokens.reshape(blocks, 128, D), preferred_element_type=jnp.float32
+    ).astype(jnp.bfloat16).reshape(rows, D)
+    cot = jnp.einsum(
+        "bst,btd->bsd",
+        onehot,
+        cotangents.reshape(blocks, 128, D),
+        preferred_element_type=jnp.float32,
+    ).reshape(rows, D)
+    gate_slot = jnp.sum(
+        jnp.where(select, gate.reshape(blocks, 1, 128), 0.0), axis=2
+    ).reshape(rows, 1)
+    pre_act = jnp.dot(picked, w_up, preferred_element_type=jnp.float32)
+    activated = activate(pre_act).astype(jnp.bfloat16)
+    result = (
+        jnp.dot(activated, w_dn, preferred_element_type=jnp.float32)
+        .astype(jnp.bfloat16)
+        .astype(jnp.float32)
+    )
+    d_gate_slot = residual_scale * jnp.sum(cot * result, axis=1)
+    d_gate = jnp.sum(jnp.where(select, d_gate_slot.reshape(blocks, CAP, 1), 0.0), axis=1)
+    gated = (gate_slot * result).astype(jnp.bfloat16)
+    mixed = jnp.einsum(
+        "bst,bsd->btd", onehot, gated.reshape(blocks, CAP, D), preferred_element_type=jnp.float32
+    ).reshape(blocks * 128, D)
+    d_result = (residual_scale * gate_slot * cot).astype(jnp.bfloat16)
+    d_act = jnp.dot(d_result, w_dn.T, preferred_element_type=jnp.float32)
+    d_down = jnp.dot(activated.T, d_result, preferred_element_type=jnp.float32)
+    d_pre = activate_backward(pre_act, d_act).astype(jnp.bfloat16)
+    d_up = jnp.dot(picked.T, d_pre, preferred_element_type=jnp.float32)
+    d_rows = jnp.dot(d_pre, w_up.T, preferred_element_type=jnp.float32).astype(jnp.bfloat16)
+    back = jnp.einsum(
+        "bst,bsd->btd", onehot, d_rows.reshape(blocks, CAP, D), preferred_element_type=jnp.float32
+    ).reshape(blocks * 128, D)
+    return (mixed, back, d_gate.reshape(blocks * 128), d_up, d_down)
+
+
 def per_device(
     layer_input,
     segment_ids,
@@ -134,17 +200,41 @@
 ):
     length = layer_input.shape[0]
     owners = lax.axis_size("expert")
+    groups = lax.axis_size("dp")
+    group_at = lax.axis_index("dp")
+    owner_at = lax.axis_index("expert")
     per_owner = w_gate_up.shape[0]
-    full_query, full_keyvalue, full_output, full_router = (
-        lax.all_gather(w_query, "dp", axis=0, tiled=True),
-        lax.all_gather(w_keyvalue, "dp", axis=0, tiled=True),
-        lax.all_gather(w_output, "dp", axis=0, tiled=True),
-        lax.all_gather(w_router, "dp", axis=0, tiled=True),
-    )
-    full_gate_up, full_down = (
-        lax.all_gather(w_gate_up, "dp", axis=1, tiled=True),
-        lax.all_gather(w_down, "dp", axis=1, tiled=True),
-    )
+    shard = w_query.shape[0]
+    part = shard // owners
+    every = ("dp", "expert")
+
+    def own_part(weight):
+        return lax.dynamic_slice_in_dim(weight, owner_at * part, part, 0)
+
+    router_rows = part * EXPERTS // D if part * EXPERTS % D == 0 else 0
+    pack = jnp.concatenate([own_part(w_query), own_part(w_keyvalue), own_part(w_output)], axis=0)
+    gathered = lax.all_gather(pack, every, axis=0).reshape(groups * owners, 3, part, D)
+    full_query = gathered[:, 0].reshape(D, HEADS * HEAD_DIM)
+    full_keyvalue = gathered[:, 1].reshape(D, 2 * KV_HEADS * HEAD_DIM)
+    full_output = gathered[:, 2].reshape(HEADS * HEAD_DIM, D)
+    full_router = lax.all_gather(own_part(w_router), every, axis=0, tiled=True)
+
+    exchange = per_owner % groups == 0
+    if exchange:
+        local = per_owner // groups
+        token_axes = ("expert", "dp")
+        first_expert = owner_at * per_owner + group_at * local
+        own_up = lax.all_to_all(w_gate_up, "dp", split_axis=0, concat_axis=1, tiled=True)
+        own_down = lax.all_to_all(w_down, "dp", split_axis=0, concat_axis=1, tiled=True)
+    else:
+        local = per_owner
+        token_axes = ("expert",)
+        first_expert = owner_at * per_owner
+        own_up = lax.all_gather(w_gate_up, "dp", axis=1, tiled=True)
+        own_down = lax.all_gather(w_down, "dp", axis=1, tiled=True)
+    all_routes = spread_over(token_axes, expert_routes)
+    all_cotangents = spread_over(token_axes, out_cotangent)
+
     cosine, sine_table = rope_tables(length, HEAD_DIM)
     places = jnp.arange(length)
     visible = (places[:, None] >= places[None, :]) & (segment_ids[:, None] == segment_ids[None, :])
@@ -159,94 +249,57 @@
     )
     normed2, inverse2 = norm_forward(hidden, second_gain)
     normed2 = normed2.astype(jnp.bfloat16)
-    logits = jnp.dot(normed2, full_router, preferred_element_type=jnp.float32)
-    chosen_mask = expert_routes[:, :, None] == jnp.arange(EXPERTS, dtype=jnp.int32)[None, None, :]
-    chosen = jnp.sum(jnp.where(chosen_mask, logits[:, None, :], 0.0), axis=2)
-    highest = jnp.max(chosen, axis=1, keepdims=True)
-    exponent = jnp.exp(chosen - highest)
-    gates = exponent / jnp.sum(exponent, axis=1, keepdims=True)
-    onehot = chosen_mask.reshape(length * TOPK, EXPERTS).astype(jnp.int32)
-    ranking = jnp.sum((jnp.cumsum(onehot, axis=0) - 1) * onehot, axis=1)
-    target = expert_routes.reshape(length * TOPK) * CAP + ranking
-    pair_slot = (
-        jnp.full((EXPERTS * CAP,), length * TOPK, jnp.int32)
-        .at[target]
-        .set(jnp.arange(length * TOPK, dtype=jnp.int32))
-    )
-    token_slot = pair_slot // TOPK
-    padded_normed = jnp.concatenate([normed2, jnp.zeros((1, D), jnp.bfloat16)], axis=0)
-    outgoing = padded_normed[token_slot].reshape(EXPERTS, CAP, D)
-    piece = lax.all_to_all(outgoing, "expert", split_axis=0, concat_axis=0, tiled=True)
-    slots = piece.shape[1]
-    grouped = piece.reshape(owners, per_owner, slots, D)
-    pre_act = jnp.einsum(
-        "sjnd,jdf->sjnf", grouped, full_gate_up, preferred_element_type=jnp.float32
-    )
-    activated = activate(pre_act).astype(jnp.bfloat16)
-    result = jnp.einsum(
-        "sjnf,jfd->sjnd", activated, full_down, preferred_element_type=jnp.float32
-    ).astype(jnp.bfloat16)
-    expert_out = result.reshape(owners * per_owner, slots, D)
-    kept_pre = pre_act.reshape(owners * per_owner, slots, 2 * F)
-    kept_act = activated.reshape(owners * per_owner, slots, F)
-    returned = lax.all_to_all(expert_out, "expert", split_axis=0, concat_axis=0, tiled=True)
-    picked = returned.reshape(EXPERTS * CAP, D)[target].reshape(length, TOPK, D).astype(jnp.float32)
-    combined = jnp.sum(gates[:, :, None] * picked, axis=1)
-    layer_output = (hidden + residual_scale * combined).astype(jnp.bfloat16)
+    all_normed2 = spread_over(token_axes, normed2)
+
+    def gates_of(rows, routes):
+        named = jnp.any(
+            routes[:, :, None] == jnp.arange(EXPERTS, dtype=jnp.int32)[None, None, :], axis=1
+        )
+        logits = jnp.dot(rows, full_router, preferred_element_type=jnp.float32)
+        highest = jnp.max(jnp.where(named, logits, -jnp.inf), axis=1, keepdims=True)
+        exponent = jnp.where(named, jnp.exp(jnp.where(named, logits - highest, 0.0)), 0.0)
+        return exponent / jnp.sum(exponent, axis=1, keepdims=True)
+
+    all_gates = gates_of(all_normed2, all_routes)
     d_out = out_cotangent.astype(jnp.float32)
-    d_gates = residual_scale * jnp.sum(picked * d_out[:, None, :], axis=2)
-    d_chosen = gates * (d_gates - jnp.sum(gates * d_gates, axis=1, keepdims=True))
-    d_logits = jnp.sum(jnp.where(chosen_mask, d_chosen[:, :, None], 0.0), axis=1).astype(
+    mixed, back = 0.0, 0.0
+    d_gate_list, up_list, down_list = [], [], []
+    for j in range(local):
+        hit = jnp.any(all_routes == first_expert + j, axis=1)
+        gate = lax.dynamic_index_in_dim(all_gates, first_expert + j, 1, keepdims=False)
+        one_mixed, one_back, d_gate, d_up, d_dn = expert_pass(
+            all_normed2, all_cotangents, gate, hit, own_up[j], own_down[j]
+        )
+        mixed, back = mixed + one_mixed, back + one_back
+        d_gate_list.append(d_gate)
+        up_list.append(d_up.astype(jnp.bfloat16))
+        down_list.append(d_dn.astype(jnp.bfloat16))
+    back_own = sum_to_owner(token_axes, back.astype(jnp.bfloat16)).astype(jnp.float32)
+    sources = EXPERTS // local
+    d_gate_out = jnp.stack(d_gate_list).reshape(local, sources, length).transpose(1, 0, 2)
+    d_gates = (
+        lax.all_to_all(d_gate_out, token_axes, split_axis=0, concat_axis=0, tiled=True)
+        .reshape(EXPERTS, length)
+        .T
+    )
+    d_up_all, d_down_all = jnp.stack(up_list), jnp.stack(down_list)
+    if exchange:
+        gate_up_grad = lax.all_to_all(d_up_all, "dp", split_axis=1, concat_axis=0, tiled=True)
+        down_grad = lax.all_to_all(d_down_all, "dp", split_axis=1, concat_axis=0, tiled=True)
+    else:
+        gate_up_grad = lax.psum_scatter(d_up_all, "dp", scatter_dimension=1, tiled=True)
+        down_grad = lax.psum_scatter(d_down_all, "dp", scatter_dimension=1, tiled=True)
+    mixed_own = sum_to_owner(token_axes, mixed.astype(jnp.bfloat16)).astype(jnp.float32)
+    layer_output = (hidden + residual_scale * mixed_own).astype(jnp.bfloat16)
+
+    gates = gates_of(normed2, expert_routes)
+    d_logits = (gates * (d_gates - jnp.sum(gates * d_gates, axis=1, keepdims=True))).astype(
         jnp.bfloat16
     )
     d_router = jnp.dot(normed2.T, d_logits, preferred_element_type=jnp.float32)
-    d_pairs = (
-        (residual_scale * gates[:, :, None] * d_out[:, None, :])
-        .astype(jnp.bfloat16)
-        .reshape(length * TOPK, D)
-    )
-    padded_pairs = jnp.concatenate([d_pairs, jnp.zeros((1, D), jnp.bfloat16)], axis=0)
-    outgoing_grad = padded_pairs[pair_slot].reshape(EXPERTS, CAP, D)
-    arrived_grad = lax.all_to_all(outgoing_grad, "expert", split_axis=0, concat_axis=0, tiled=True)
-    grouped_grad = arrived_grad.reshape(owners, per_owner, CAP, D)
-    grouped_rows = piece.reshape(owners, per_owner, CAP, D)
-    pre_act = kept_pre.reshape(owners, per_owner, CAP, 2 * F)
-    activated = kept_act.reshape(owners, per_owner, CAP, F)
-    d_act = jnp.einsum(
-        "sjnd,jfd->sjnf", grouped_grad, full_down, preferred_element_type=jnp.float32
-    )
-    d_down = jnp.einsum(
-        "sjnf,sjnd->jfd", activated, grouped_grad, preferred_element_type=jnp.float32
-    )
-    d_pre = activate_backward(pre_act, d_act).astype(jnp.bfloat16)
-    d_gate_up = jnp.einsum(
-        "sjnd,sjnf->jdf", grouped_rows, d_pre, preferred_element_type=jnp.float32
-    )
-    d_rows = jnp.einsum(
-        "sjnf,jdf->sjnd", d_pre, full_gate_up, preferred_element_type=jnp.float32
-    ).astype(jnp.bfloat16)
-    back_rows = lax.all_to_all(
-        d_rows.reshape(owners * per_owner, CAP, D),
-        "expert",
-        split_axis=0,
-        concat_axis=0,
-        tiled=True,
-    )
-    gate_up_grad, down_grad = (
-        lax.psum_scatter(
-            d_gate_up.astype(jnp.bfloat16), "dp", scatter_dimension=1, tiled=True
-        ).astype(jnp.float32),
-        lax.psum_scatter(d_down.astype(jnp.bfloat16), "dp", scatter_dimension=1, tiled=True).astype(
-            jnp.float32
-        ),
-    )
-    gathered_back = (
-        back_rows.reshape(EXPERTS * CAP, D)[target].reshape(length, TOPK, D).astype(jnp.float32)
-    )
-    d_normed2 = jnp.sum(gathered_back, axis=1) + jnp.dot(
-        d_logits, full_router.T, preferred_element_type=jnp.float32
-    )
+    d_normed2 = back_own + jnp.dot(d_logits, full_router.T, preferred_element_type=jnp.float32)
     d_second_gain, d_through = norm_backward(hidden, inverse2, second_gain, d_normed2)
+    second_gain_grad = butterfly_sum(d_second_gain, ("expert", "dp"))
     d_hidden = d_out + d_through
     d_branch = (residual_scale * d_hidden).astype(jnp.bfloat16)
     d_wout = jnp.dot(attended.T, d_branch, preferred_element_type=jnp.float32)
@@ -273,28 +326,21 @@
         d_keyvalue, full_keyvalue.T, preferred_element_type=jnp.float32
     )
     d_first_gain, d_inputs = norm_backward(inputs_f32, inverse, first_gain, d_normed)
+    first_gain_grad = butterfly_sum(d_first_gain, ("expert", "dp"))
     input_grad = (d_hidden + d_inputs).astype(jnp.bfloat16)
-    share_query, share_keyvalue, share_output, share_router = (
-        lax.psum_scatter(
-            d_wquery.astype(jnp.bfloat16), "dp", scatter_dimension=0, tiled=True
-        ).astype(jnp.float32),
-        lax.psum_scatter(
-            d_wkeyvalue.astype(jnp.bfloat16), "dp", scatter_dimension=0, tiled=True
-        ).astype(jnp.float32),
-        lax.psum_scatter(d_wout.astype(jnp.bfloat16), "dp", scatter_dimension=0, tiled=True).astype(
-            jnp.float32
-        ),
-        lax.psum_scatter(
-            d_router.astype(jnp.bfloat16), "dp", scatter_dimension=0, tiled=True
-        ).astype(jnp.float32),
-    )
-    query_grad, keyvalue_grad, output_grad, router_grad = (
-        lax.psum(share_query.astype(jnp.bfloat16), "expert").astype(jnp.float32),
-        lax.psum(share_keyvalue.astype(jnp.bfloat16), "expert").astype(jnp.float32),
-        lax.psum(share_output.astype(jnp.bfloat16), "expert").astype(jnp.float32),
-        lax.psum(share_router.astype(jnp.bfloat16), "expert").astype(jnp.float32),
-    )
-    first_gain_grad, second_gain_grad = lax.psum((d_first_gain, d_second_gain), ("dp", "expert"))
+
+    def reduced(*grads):
+        packed = jnp.stack([g.astype(jnp.bfloat16) for g in grads])
+        count, width = len(grads), grads[0].shape[1]
+        packed = packed.reshape(count, groups, owners, part, width).transpose(2, 1, 0, 3, 4)
+        packed = packed.reshape(owners * groups * count * part, width)
+        mine = sum_to_owner(("expert", "dp"), packed).reshape(1, count, part, width)
+        whole = lax.all_gather(mine, "expert", axis=0, tiled=True)
+        whole = whole.transpose(1, 0, 2, 3).reshape(count, owners * part, width)
+        return [whole[i].astype(jnp.float32) for i in range(count)]
+
+    output_grad, query_grad, keyvalue_grad = reduced(d_wout, d_wquery, d_wkeyvalue)
+    (router_grad,) = reduced(d_router)
     return (
         layer_output,
         input_grad,
@@ -304,8 +350,8 @@
         output_grad,
         second_gain_grad,
         router_grad,
-        gate_up_grad,
-        down_grad,
+        gate_up_grad.astype(jnp.float32),
+        down_grad.astype(jnp.float32),
     )
 
 

time: 957 us -> 755 us (0.79)
  waiting for transfers between devices: 688 us -> 407 us
  blocking collectives: 79.1 us -> 113 us
  local copies, waits for them, and re-layouts: 41 us -> 56.9 us
  starting transfers between devices: 17.4 us -> 32.7 us
  other arithmetic: 37.8 us -> 47.5 us
    all_gather x5 -> x6, waiting for transfers between devices: 289 us -> 108 us  [the longest x1 69.5 us: per_device(): lax.all_gather(pack, every, axis=0).reshape(groups * owners, 3, part, D)]
    all_gather x1 -> x4, blocking collectives: 15.7 us -> 113 us  [the longest x2 62.4 us: spread_over(): array = lax.all_gather(array, axis, axis=0, tiled=True)]
    reduce_scatter x6 -> x7, waiting for transfers between devices: 339 us -> 270 us  [sum_to_owner(): array = lax.psum_scatter(array, axis, scatter_dimension=0, tiled=True)]
    psum x2 -> x0, blocking collectives: 63.4 us -> none  [the longest x1 39.6 us: per_device(): lax.psum((d_first_gain, d_second_gain), ('dp', 'expert'))]
    all_to_all x4 -> x5, waiting for transfers between devices: 57.1 us -> 18.5 us  [the longest x1 11.6 us: per_device(): lax.all_to_all(w_down, 'dp', split_axis=0, concat_axis=1, tiled=True)]
    unnamed x85 -> x106, local copies, waits for them, and re-layouts: 6.25 us -> 31.1 us
    gather x4 -> x0, local copies, waits for them, and re-layouts: 22.8 us -> none  [the longest x1 7.09 us: per_device(): returned.reshape(EXPERTS * CAP, D)[target].reshape(length, TOPK, D)]
    unnamed x0 -> x3, other arithmetic: none -> 20.7 us
  transfers between devices with their start and end apart: 16 -> 29, of which waited for: 13 -> 16; matrix products, arithmetic and copies ran while one was open for 10% -> 16% of each run, Pallas kernels for 0% -> 0%
where the time goes in v1:
time: 755 us; the launch traced here: 747 us
  waiting for transfers between devices  407 us (54%)
  blocking collectives  113 us (15%)
  matrix products  74.6 us (10%)
  local copies, waits for them, and re-layouts  56.9 us (8%)
  other arithmetic  47.5 us (6%)
  starting transfers between devices  32.7 us (4%)
  between operations  15.3 us (2%)
    reduce_scatter x7, waiting for transfers between devices, sum_to_owner(): array = lax.psum_scatter(array, axis, scatter_dimension=0, tiled=True)  270 us
    all_gather x1, waiting for transfers between devices, per_device(): lax.all_gather(pack, every, axis=0).reshape(groups * owners, 3, part, D)  69.5 us
    all_gather x2, blocking collectives, spread_over(): array = lax.all_gather(array, axis, axis=0, tiled=True)  62.4 us
    all_gather x1, blocking collectives, per_device(): full_router = lax.all_gather(own_part(w_router), every, axis=0, tiled=True)  40.9 us
    all_gather x4, waiting for transfers between devices, spread_over(): array = lax.all_gather(array, axis, axis=0, tiled=True)  38.1 us
    unnamed x106, local copies, waits for them, and re-layouts  31.1 us
    unnamed x3, other arithmetic  20.7 us
  transfers between devices with their start and end apart: 29, of which 16 were waited for; matrix products, arithmetic and copies ran while one was open for 16% of the time, Pallas kernels for 0%

profile of v1, /device:TPU:0, one launch (start us, length us, event | category | flops | bytes accessed | tf_op | source)
XLA Modules:
  0.0 747.2 jit_solution(1612328356456202921)
XLA Ops:
  13.9 69.5 %all-gather.19.cloned.1.call-done = bf16[3072,1024]{1,0:T(8,128)(2,1)} async-done(((bf16[96,1024]{1,0:T(8,128)(2,1)}), bf16[3072,1024]{1,0:T(8,128)(2,1)}) %all-gather.19.cloned.1.call-update) | async-done | bytes 6291472 | tf_op jit(solution)/shard_map/all_gather | solution.py:216
  83.4 6.1 fusion.64
  89.4 2.6 copy.77
  92.1 2.4 fusion.39
  95.3 2.9 copy.78
  102.9 8.6 %all-gather.13.cloned.1.call-done = bf16[512,1024]{1,0:T(8,128)(2,1)} async-done(((bf16[128,1024]{1,0:T(8,128)(2,1)}), bf16[512,1024]{1,0:T(8,128)(2,1)}) %all-gather.13.cloned.1.call-update) | async-done | bytes 1048592 | tf_op jit(solution)/shard_map/all_gather | solution.py:133
  111.6 29.5 %all-gather.9.cloned.1.call-done = bf16[512,1024]{1,0:T(8,128)(2,1)} async-done(((bf16[128,1024]{1,0:T(8,128)(2,1)}), bf16[512,1024]{1,0:T(8,128)(2,1)}) %all-gather.9.cloned.1.call-update) | async-done | bytes 1048592 | tf_op jit(solution)/shard_map/all_gather | solution.py:133
  141.1 4.5 all-to-all-start
  145.7 53.3 %all_gather.35 = s32[512,8]{0,1:T(8,128)S(1)} all-gather(s32[128,8]{0,1:T(8,128)S(1)} %copy-done.37), channel_id=1, replica_groups=mesh['dp'=4,'expert'=8] {'dp'}, dimensions={0}, use_global_device_ids=true | all-gather | bytes 20480 | tf_op jit(solution)/shard_map/all_gather | solution.py:133
  199.0 9.2 %all_gather.36 = s32[4096,8]{0,1:T(8,128)S(1)} all-gather(s32[512,8]{0,1:T(8,128)S(1)} %all_gather.35), channel_id=1, replica_groups=mesh['dp'=4,'expert'=8] {'expert'}, dimensions={0}, use_global_device_ids=true | all-gather | bytes 147456 | tf_op jit(solution)/shard_map/all_gather | solution.py:133
  208.5 40.9 %all_gather.39 = bf16[1024,32]{1,0:T(8,128)(2,1)S(1)} all-gather(bf16[32,32]{1,0:T(8,128)(2,1)S(1)} %copy.120), channel_id=1, replica_groups=mesh['dp'=4,'expert'=8] {'dp','expert'}, dimensions={0}, use_global_device_ids=true | all-gather | bytes 67584 | tf_op jit(solution)/shard_map/all_gather | solution.py:220
  250.1 7.0 fusion.13
  257.1 3.5 all-to-all-start.1
  260.9 4.6 convolution_convert_fusion.4
  265.6 5.7 fusion.67
  271.3 2.4 copy-done.8
  273.7 1.9 multiply_convert_fusion.3
  275.5 11.6 %all-to-all-done.1 = bf16[4,128,1024]{2,1,0:T(8,128)(2,1)S(1)} async-done(((bf16[4,128,1024]{2,1,0:T(8,128)(2,1)}), bf16[4,128,1024]{2,1,0:T(8,128)(2,1)S(1)}, u32[]{:S(2)}, u32[]{:S(2)}) %all-to-all-start.1) | async-done | bytes 1048608 | tf_op jit(solution)/shard_map/all_to_all | solution.py:228
  287.1 6.3 fusion.1
  293.6 6.1 select_reduce_fusion.2
  301.2 2.1 copy-done.9
  303.6 2.3 multiply_convert_fusion.2
  305.9 5.7 convolution_convert_fusion.3
  311.7 5.7 convolution_convert_fusion
  317.5 2.2 fusion
  319.8 7.0 convolution_convert_fusion.1
  326.9 59.4 %reduce-scatter.17.cloned.1.call-done = bf16[512,1024]{1,0:T(8,128)(2,1)} async-done(((bf16[4096,1024]{1,0:T(8,128)(2,1)}), bf16[512,1024]{1,0:T(8,128)(2,1)}) %reduce-scatter.17.cloned.1.call-update) | async-done | bytes 1048592 | tf_op jit(solution)/shard_map/reduce_scatter | solution.py:139
  386.3 74.9 %reduce-scatter.13.cloned.1.call-done = bf16[512,1024]{1,0:T(8,128)(2,1)} async-done(((bf16[4096,1024]{1,0:T(8,128)(2,1)}), bf16[512,1024]{1,0:T(8,128)(2,1)}) %reduce-scatter.13.cloned.1.call-update) | async-done | bytes 1048592 | tf_op jit(solution)/shard_map/reduce_scatter | solution.py:139
  461.5 4.6 all-to-all-start.2
  466.4 6.9 all-to-all-done.2
  473.3 17.5 %reduce-scatter.19.cloned.1.call-done = bf16[128,1024]{1,0:T(8,128)(2,1)} async-done(((bf16[512,1024]{1,0:T(8,128)(2,1)}), bf16[128,1024]{1,0:T(8,128)(2,1)}) %reduce-scatter.19.cloned.1.call-update) | async-done | bytes 262160 | tf_op jit(solution)/shard_map/reduce_scatter | solution.py:139
  490.8 1.9 multiply_reduce_fusion
  492.8 26.2 %reduce-scatter.15.cloned.1.call-done = bf16[128,1024]{1,0:T(8,128)(2,1)} async-done(((bf16[512,1024]{1,0:T(8,128)(2,1)}), bf16[128,1024]{1,0:T(8,128)(2,1)}) %reduce-scatter.15.cloned.1.call-update) | async-done | bytes 262160 | tf_op jit(solution)/shard_map/reduce_scatter | solution.py:139
  519.0 2.1 subtract_add_fusion
  521.0 3.2 convolution_convert_fusion.9
  531.0 3.4 copy.110
  535.1 2.9 fusion.2
  538.1 1.5 fusion.4
  539.6 1.6 copy.124
  541.8 7.9 %reduce.3 = bf16[512,1024]{1,0:T(8,128)(2,1)} reduce(bf16[512,1,1024]{2,1,0:T(2,128)(2,1)S(1)} %bitcast.217, bf16[]{:T(256)} %broadcast.175), dimensions={1}, to_apply=%bitcast.197.reduce_sub_computation | reduce | bytes 2097154
  549.7 3.7 reshape.332
  553.4 4.4 all-to-all-start.4
  559.3 35.5 %reduce-scatter.21.cloned.1.call-done = bf16[384,1024]{1,0:T(8,128)(2,1)} async-done(((bf16[3072,1024]{1,0:T(8,128)(2,1)}), bf16[384,1024]{1,0:T(8,128)(2,1)}) %reduce-scatter.21.cloned.1.call-update) | async-done | bytes 786448 | tf_op jit(solution)/shard_map/reduce_scatter | solution.py:139
  594.9 5.0 convert_bitcast_fusion
  599.9 5.2 copy.123
  605.1 12.7 %reduce.2 = bf16[1024,1024]{1,0:T(8,128)(2,1)S(1)} reduce(bf16[1024,1,1024]{2,1,0:T(2,128)(2,1)} %bitcast.214, bf16[]{:T(256)} %broadcast.175), dimensions={1}, to_apply=%bitcast.196.reduce_sub_computation | reduce | bytes 4194306
  617.9 2.8 reshape.330
  620.7 4.7 all-to-all-start.3
  625.4 6.7 reduce-scatter.25.cloned.1.call-done
  632.2 46.9 %reduce-scatter.23.cloned.1.call-done = bf16[96,1024]{1,0:T(8,128)(2,1)} async-done(((bf16[384,1024]{1,0:T(8,128)(2,1)}), bf16[96,1024]{1,0:T(8,128)(2,1)}) %reduce-scatter.23.cloned.1.call-update) | async-done | bytes 196624 | tf_op jit(solution)/shard_map/reduce_scatter | solution.py:139
  680.6 2.4 fusion.69
  683.0 1.7 fusion.23
  685.2 1.5 collective-permute-start.6
  688.8 1.5 collective-permute-start.7
  691.1 9.7 %reduce-scatter.27.cloned.1.call-done = bf16[32,32]{1,0:T(8,128)(2,1)} async-done(((bf16[128,32]{1,0:T(8,128)(2,1)}), bf16[32,32]{1,0:T(8,128)(2,1)}) %reduce-scatter.27.cloned.1.call-update) | async-done | bytes 2064 | tf_op jit(solution)/shard_map/reduce_scatter | solution.py:139
  700.8 9.6 %all-gather.1 = bf16[256,32]{1,0:T(8,128)(2,1)S(1)} all-gather(bf16[32,32]{1,0:T(8,128)(2,1)} %reduce-scatter.27.cloned.1.call-done), channel_id=3, replica_groups=mesh['dp'=4,'expert'=8] {'expert'}, dimensions={0}, use_global_device_ids=true | all-gather | bytes 18432 | tf_op jit(solution)/shard_map/all_gather | solution.py:338
  711.1 2.6 reshape.333
  713.7 1.8 copy.119
  715.5 5.1 reshape.331
  720.6 5.3 copy.118
  726.0 2.0 collective-permute-start.3
  728.0 1.6 collective-permute-done.8
  730.0 2.5 collective-permute-start.4
  735.2 1.6 fusion.65
  (225 shorter events, 37.9 us)
Async XLA Ops:
  7.2 76.2 %all-gather.19.cloned.1.call-start = ((), (), s32[]{:S(2)}) async-start(), calls=%async_computation.24 | async-start | bytes 6488064 | tf_op jit(solution)/shard_map/all_gather | solution.py:216
  9.8 101.6 %all-gather.13.cloned.1.call-start = ((), (), s32[]{:S(2)}) async-start(), calls=%async_computation.17 | async-start | bytes 1310720 | tf_op jit(solution)/shard_map/all_gather | solution.py:133
  10.6 130.4 %all-gather.9.cloned.1.call-start = ((), (), s32[]{:S(2)}) async-start(), calls=%async_computation.13 | async-start | bytes 1310720 | tf_op jit(solution)/shard_map/all_gather | solution.py:133
  12.3 85.9 %copy-start.34 = (f32[128]{0:T(128)}, f32[128]{0:T(128)S(1)}, u32[]{:S(2)}) copy-start(f32[128]{0:T(128)S(1)} %get-tuple-element.61) | copy-start | bytes 1540
  13.8 85.2 %copy-start.22 = (f32[128,64]{0,1:T(8,128)}, f32[128,64]{0,1:T(8,128)S(1)}, u32[]{:S(2)}) copy-start(f32[128,64]{0,1:T(8,128)S(1)} %get-tuple-element.80) | copy-start | bytes 98308
  89.4 5.0 copy-start.2
  89.4 2.6 copy-start.5
  89.4 2.6 copy-start.28
  94.5 5.4 copy-start.11
  100.2 11.3 %copy-start.16 = (bf16[8,64,2,128]{3,1,2,0:T(8,128)(2,1)}, bf16[8,64,2,128]{3,1,2,0:T(8,128)(2,1)S(1)}, u32[]{:S(2)}) copy-start(bf16[8,64,2,128]{3,1,2,0:T(8,128)(2,1)S(1)} %convolution_convert_fusion.10) | copy-start | bytes 786436
  101.4 389.5 %copy-start.6 = (f32[128,1024]{1,0:T(8,128)}, f32[128,1024]{1,0:T(8,128)S(1)}, u32[]{:S(2)}) copy-start(f32[128,1024]{1,0:T(8,128)S(1)} %get-tuple-element.69) | copy-start | bytes 1572868
  102.0 39.1 %copy-start.39 = (f32[128]{0:T(128)}, f32[128]{0:T(128)S(1)}, u32[]{:S(2)}) copy-start(f32[128]{0:T(128)S(1)} %get-tuple-element.63) | copy-start | bytes 1540
  102.8 147.3 %all-gather.15.cloned.1.call-start = ((), (), s32[]{:S(2)}) async-start(), calls=%async_computation.18 | async-start | bytes 9437184 | tf_op jit(solution)/shard_map/all_gather | solution.py:133
  111.5 149.4 %all-gather.11.cloned.1.call-start = ((), (), s32[]{:S(2)}) async-start(), calls=%async_computation.14 | async-start | bytes 9437184 | tf_op jit(solution)/shard_map/all_gather | solution.py:133
  141.0 4.5 copy-start.41
  141.0 4.7 copy-start.37
  141.1 116.1 %all-to-all-start = ((bf16[4,256,1024]{2,1,0:T(8,128)(2,1)}), bf16[4,256,1024]{2,1,0:T(8,128)(2,1)}, u32[]{:S(2)}, u32[]{:S(2)}) async-start(bf16[4,256,1024]{2,1,0:T(8,128)(2,1)} %param.21), calls=%async_computation | async-start | bytes 4194304 | tf_op jit(solution)/shard_map/all_to_all | solution.py:227
  257.1 30.0 %all-to-all-start.1 = ((bf16[4,128,1024]{2,1,0:T(8,128)(2,1)}), bf16[4,128,1024]{2,1,0:T(8,128)(2,1)S(1)}, u32[]{:S(2)}, u32[]{:S(2)}) async-start(bf16[4,128,1024]{2,1,0:T(8,128)(2,1)} %param.22), calls=%async_computation.1 | async-start | bytes 2097152 | tf_op jit(solution)/shard_map/all_to_all | solution.py:228
  260.6 125.6 %reduce-scatter.17.cloned.1.call-start = ((), (), s32[]{:S(2)}) async-start(), calls=%async_computation.19 | async-start | bytes 9437184 | tf_op jit(solution)/shard_map/reduce_scatter | solution.py:139
  265.5 5.7 copy-start.18
  287.1 6.3 copy-start.13
  293.5 7.4 slice-start
  293.6 7.3 slice-start.1
  300.8 2.5 copy-start.9
  300.9 2.8 copy-start.14
  305.9 5.7 copy-start.43
  305.9 5.7 copy-start.45
  317.4 143.9 %reduce-scatter.13.cloned.1.call-start = ((), (), s32[]{:S(2)}) async-start(), calls=%async_computation.15 | async-start | bytes 9437184 | tf_op jit(solution)/shard_map/reduce_scatter | solution.py:139
  326.8 134.5 %copy-start.38 = (s32[128,8]{0,1:T(8,128)S(1)}, s32[128,8]{0,1:T(8,128)}, u32[]{:S(2)}) copy-start(s32[128,8]{0,1:T(8,128)} %param.14) | copy-start | bytes 12292
  326.8 134.5 %copy-start.15 = (bf16[128,1024]{1,0:T(8,128)(2,1)S(1)}, bf16[128,1024]{1,0:T(8,128)(2,1)}, u32[]{:S(2)}) copy-start(bf16[128,1024]{1,0:T(8,128)(2,1)} %multiply_convert_fusion.5) | copy-start | bytes 786436
  326.8 164.0 %copy-start.40 = (f32[128]{0:T(128)S(1)}, f32[128]{0:T(128)}, u32[]{:S(2)}) copy-start(f32[128]{0:T(128)} %copy-done.39) | copy-start | bytes 1540
  326.8 192.1 %copy-start.24 = (bf16[128,1024]{1,0:T(8,128)(2,1)S(1)}, bf16[128,1024]{1,0:T(8,128)(2,1)}, u32[]{:S(2)}) copy-start(bf16[128,1024]{1,0:T(8,128)(2,1)} %param.23) | copy-start | bytes 786436
  326.8 164.0 %reduce-scatter.19.cloned.1.call-start = ((), (), s32[]{:S(2)}) async-start(), calls=%async_computation.20 | async-start | bytes 1310720 | tf_op jit(solution)/shard_map/reduce_scatter | solution.py:139
  386.3 132.7 %reduce-scatter.15.cloned.1.call-start = ((), (), s32[]{:S(2)}) async-start(), calls=%async_computation.16 | async-start | bytes 1310720 | tf_op jit(solution)/shard_map/reduce_scatter | solution.py:139
  461.5 11.7 %all-to-all-start.2 = ((f32[32,1,128]{2,1,0:T(1,128)}), f32[32,1,128]{2,1,0:T(1,128)S(1)}, u32[]{:S(2)}, u32[]{:S(2)}) async-start(f32[32,1,128]{2,1,0:T(1,128)} %bitcast.36), calls=%async_computation.6 | async-start | bytes 32768 | tf_op jit(solution)/shard_map/all_to_all | solution.py:281
  466.2 128.7 %reduce-scatter.21.cloned.1.call-start = ((), (), s32[]{:S(2)}) async-start(), calls=%async_computation.21 | async-start | bytes 7077888 | tf_op jit(solution)/shard_map/reduce_scatter | solution.py:139
  473.3 45.6 %copy-start.31 = (bf16[128,32]{0,1:T(8,128)(2,1)}, bf16[128,32]{0,1:T(8,128)(2,1)S(1)}, u32[]{:S(2)}) copy-start(bf16[128,32]{0,1:T(8,128)(2,1)S(1)} %multiply_convert_fusion.8) | copy-start | bytes 24580
  519.0 6.4 copy-start.17
  521.0 4.8 copy-start.12
  535.1 2.9 copy-start.10
  549.7 8.2 %copy-start.32 = (bf16[128,32]{0,1:T(8,128)(2,1)S(1)}, bf16[128,32]{0,1:T(8,128)(2,1)}, u32[]{:S(2)}) copy-start(bf16[128,32]{0,1:T(8,128)(2,1)} %copy-done.31) | copy-start | bytes 24580
  553.4 41.4 %copy-start.44 = (bf16[1280,512]{0,1:T(8,128)(2,1)S(1)}, bf16[1280,512]{0,1:T(8,128)(2,1)}, u32[]{:S(2)}) copy-start(bf16[1280,512]{0,1:T(8,128)(2,1)} %copy-done.43) | copy-start | bytes 3932164
  553.4 67.3 %all-to-all-start.4 = ((bf16[4,2,65536]{2,1,0:T(2,128)(2,1)}), bf16[4,2,65536]{2,1,0:T(2,128)(2,1)}, u32[]{:S(2)}, u32[]{:S(2)}) async-start(bf16[4,2,65536]{2,1,0:T(2,128)(2,1)} %reshape.332), calls=%async_computation.10 | async-start | bytes 2097152 | tf_op jit(solution)/shard_map/all_to_all | solution.py:288
  557.8 74.3 %reduce-scatter.25.cloned.1.call-start = ((), (), s32[]{:S(2)}) async-start(), calls=%async_computation.25 | async-start | bytes 294912
  559.3 119.9 %reduce-scatter.23.cloned.1.call-start = ((), (), s32[]{:S(2)}) async-start(), calls=%async_computation.22 | async-start | bytes 983040 | tf_op jit(solution)/shard_map/reduce_scatter | solution.py:139
  620.7 58.5 %copy-start.36 = (f32[1024]{0:T(1024)S(1)}, f32[1024]{0:T(1024)}, u32[]{:S(2)}) copy-start(f32[1024]{0:T(1024)} %get-tuple-element.30) | copy-start | bytes 12292
  620.7 58.6 %copy-start.26 = (f32[128,64]{0,1:T(8,128)S(1)}, f32[128,64]{0,1:T(8,128)}, u32[]{:S(2)}) copy-start(f32[128,64]{0,1:T(8,128)} %get-tuple-element.58) | copy-start | bytes 98308
  620.7 94.8 %all-to-all-start.3 = ((bf16[4,2,131072]{2,1,0:T(2,128)(2,1)}), bf16[4,2,131072]{2,1,0:T(2,128)(2,1)}, u32[]{:S(2)}, u32[]{:S(2)}) async-start(bf16[4,2,131072]{2,1,0:T(2,128)(2,1)} %reshape.330), calls=%async_computation.9 | async-start | bytes 4194304 | tf_op jit(solution)/shard_map/all_to_all | solution.py:287
  625.4 57.6 %copy-start.3 = (bf16[32,1,32,1024]{3,2,1,0:T(8,128)(2,1)S(1)}, bf16[32,1,32,1024]{3,2,1,0:T(8,128)(2,1)}, u32[]{:S(2)}) copy-start(bf16[32,1,32,1024]{3,2,1,0:T(8,128)(2,1)} %copy-done.2) | copy-start | bytes 6291460
  625.4 75.4 %reduce-scatter.27.cloned.1.call-start = ((), (), s32[]{:S(2)}) async-start(), calls=%async_computation.26 | async-start | bytes 40960 | tf_op jit(solution)/shard_map/reduce_scatter | solution.py:139
  632.2 103.1 %all-gather.17.cloned.1.call-start = ((), (), s32[]{:S(2)}) async-start(), calls=%async_computation.23 | async-start | bytes 1769472 | tf_op jit(solution)/shard_map/all_gather | solution.py:338
  679.2 6.0 collective-permute-start.5
  684.7 2.0 collective-permute-start
  685.2 3.6 collective-permute-start.6
  686.7 3.6 collective-permute-start.1
  688.8 37.1 %collective-permute-start.7 = (f32[1024]{0:T(1024)S(1)}, f32[1024]{0:T(1024)S(1)}, u32[]{:S(2)}, u32[]{:S(2)}) collective-permute-start(f32[1024]{0:T(1024)S(1)} %add.160), channel_id=1, source_target_pairs={{0,4},{1,5},{2,6},{3,7},{4,0},{5,1},{6,2},{7,3},{8,12},{9,13},{10,... | collective-permute-start | bytes 12296 | tf_op jit(solution)/shard_map/ppermute | solution.py:126
  690.3 35.7 %collective-permute-start.2 = (f32[1024]{0:T(1024)S(1)}, f32[1024]{0:T(1024)S(1)}, u32[]{:S(2)}, u32[]{:S(2)}) collective-permute-start(f32[1024]{0:T(1024)S(1)} %add.154), channel_id=1, source_target_pairs={{0,4},{1,5},{2,6},{3,7},{4,0},{5,1},{6,2},{7,3},{8,12},{9,13},{10,... | collective-permute-start | bytes 12296 | tf_op jit(solution)/shard_map/ppermute | solution.py:126
  720.6 11.8 %copy-start.21 = (f32[128,1024]{1,0:T(8,128)S(1)}, f32[128,1024]{1,0:T(8,128)}, u32[]{:S(2)}) copy-start(f32[128,1024]{1,0:T(8,128)} %get-tuple-element.77) | copy-start | bytes 1572868
  720.6 11.9 %copy-start.42 = (f32[128]{0:T(128)S(1)}, f32[128]{0:T(128)}, u32[]{:S(2)}) copy-start(f32[128]{0:T(128)} %get-tuple-element.60) | copy-start | bytes 1540
  725.9 3.6 collective-permute-start.8
  726.0 4.0 collective-permute-start.3
  729.5 4.5 collective-permute-start.9
  730.0 4.7 collective-permute-start.4
  735.2 4.9 copy-start.1
  (13 other events, 19.6 us)
Sparse Core Ops, SparseCore 0:
  11.4 71.8 all-gather.18
  84.9 26.5 all-gather.12
  113.6 27.3 all-gather.8
  142.8 53.6 all-gather.14
  198.2 55.5 all-gather.10
  317.5 68.7 reduce-scatter.16
  389.7 71.4 reduce-scatter.12
  463.5 27.2 reduce-scatter.18
  493.1 25.7 reduce-scatter.14
  534.5 60.2 reduce-scatter.20
  598.4 33.6 reduce-scatter.24
  634.3 44.8 reduce-scatter.22
  681.4 19.3 reduce-scatter.26
  702.5 23.6 all-gather.16
